TPU v7x, 512 devices: a whole 4x8x8 slice. The times are simulated.
512 devices in a mesh: loop: 16 (over x, y_lo, core), groups: 32 (over y_hi, z).
Axes of the slice: x: 4, y: 8 (y_hi: 4, y_lo: 2; y = y_hi * 2 + y_lo), z: 8, core: 2. Of those that a mesh axis runs over, the one named last changes fastest.
Arguments:
- states: bfloat16 [65536, 1024], P(('loop', 'groups')), may hold values from -64 to 64
- premises: bfloat16 [65536, 1024], P(('loop', 'groups')), may hold values from -1 to 1
- counts: int32 [16, 32], P('loop', 'groups'), may hold values from 64 to 128, as said below
- partner_mask: int32 [16], P('loop'), may hold values from 0 to 31, as said below
- send_rows: int32 [16, 32, 16], P('loop', 'groups'), may hold values from 0 to 63
- hard_idx: int32 [65536], P(('loop', 'groups')), may hold values from 0 to 15
Outputs:
- loss: float32 [], replicated
- grad_states: bfloat16 [65536, 1024], P(('loop', 'groups'))
- grad_premises: bfloat16 [65536, 1024], P(('loop', 'groups'))
Inputs may be any that keep to these rules, and one draw needn't show every extreme that they name: `counts`: at least 64 valid pairs on every device; some device has all slots valid. `partner_mask`: loop index 0 has the value 32 // 2.
All inputs are finite; a program needn't handle non-finite values.
Results may differ from a plain program's by a relative error of at most 0.0034.
Values may be sent and summed in bfloat16 or wider, within the bound.
A program may use at most 64 MiB of HBM per device.

v0:
```python
import jax
import jax.numpy as jnp
from jax import lax
from jax.sharding import PartitionSpec as P

SCALE = 3.0


def from_behind(value, axis, steps):
    count = lax.axis_size(axis)
    pairs = [(source, (source + steps) % count) for source in range(count)]
    return lax.ppermute(value, axis, pairs)


def body(states, premises, counts, partner_mask, send_rows, hard_idx):
    rows = states.shape[0]
    offer = send_rows.shape[2]
    loop_size = lax.axis_size("loop")
    group_size = lax.axis_size("groups")
    here = lax.axis_index("loop")
    group = lax.axis_index("groups")
    slots = jnp.arange(rows, dtype=jnp.int32)
    valid = slots < counts[0, 0]
    vflt = valid.astype(jnp.float32)
    partner = jnp.bitwise_xor(group, partner_mask[0])
    keys, counts_all = (
        lax.all_gather(premises, "loop", axis=0, tiled=True),
        lax.all_gather(counts, "loop", axis=0, tiled=True),
    )
    column = jnp.arange(loop_size * rows, dtype=jnp.int32)
    limits = jnp.repeat(counts_all[:, 0], rows)
    key_ok = column % rows < limits
    scores = SCALE * jnp.einsum("pd,kd->pk", states, keys, preferred_element_type=jnp.float32)
    masked = jnp.where(key_ok[None, :], scores, -jnp.inf)
    top = jnp.max(masked, axis=1)
    lse = top + jnp.log(jnp.sum(jnp.exp(masked - top[:, None]), axis=1))
    own_block = lax.dynamic_slice_in_dim(scores, here * rows, rows, 1)
    pos = jnp.diagonal(own_block)
    offered = premises[send_rows[0, 0]]
    piece = lax.all_gather(offered, "groups", axis=0, tiled=True)
    offset = partner * offer
    count = piece.shape[0]
    inside = jnp.logical_and(offset >= 0, offset < count)
    part = lax.dynamic_slice_in_dim(piece, jnp.clip(offset, 0, count - offer), offer, 0)
    pool = jnp.where(inside, part, jnp.zeros_like(offered))
    hard = pool[hard_idx]
    states_f = states.astype(jnp.float32)
    hard_f = hard.astype(jnp.float32)
    tval = SCALE * jnp.sum(states_f * hard_f, axis=-1)
    qval = jnp.where(valid, jax.nn.sigmoid(tval - pos), 0.0)
    terms = jnp.where(valid, lse - pos + jax.nn.softplus(tval - pos), 0.0)
    loss = lax.psum(jnp.sum(terms), ("loop", "groups")) / (loop_size * group_size * rows)
    prob = jnp.where(valid[:, None], jnp.exp(masked - lse[:, None]), 0.0).astype(jnp.bfloat16)
    dstate = jnp.dot(prob, keys, preferred_element_type=jnp.float32)
    grad_states = SCALE * (
        dstate + qval[:, None] * hard_f - (vflt + qval)[:, None] * premises.astype(jnp.float32)
    )

    def visit(step, carry):
        block = jnp.remainder(here - step, loop_size)
        columns = lax.dynamic_slice_in_dim(prob, block * rows, rows, 1)
        carry = carry + jnp.einsum("pk,pd->kd", columns, states, preferred_element_type=jnp.float32)
        return from_behind(carry.astype(jnp.bfloat16), "loop", 1).astype(carry.dtype)

    dprem = lax.fori_loop(0, loop_size, visit, jnp.zeros(states.shape, jnp.float32))
    pick = jax.nn.one_hot(hard_idx, offer, dtype=jnp.float32)
    back = SCALE * jnp.dot(pick.T, qval[:, None] * states_f, precision=lax.Precision.HIGHEST)
    piece = lax.all_gather(back, "groups", axis=0, tiled=True)
    offset = partner * offer
    count = piece.shape[0]
    inside = jnp.logical_and(offset >= 0, offset < count)
    part = lax.dynamic_slice_in_dim(piece, jnp.clip(offset, 0, count - offer), offer, 0)
    back_home = jnp.where(inside, part, jnp.zeros_like(back))
    place = jax.nn.one_hot(send_rows[0, 0], rows, dtype=jnp.float32)
    dhard = jnp.dot(place.T, back_home, precision=lax.Precision.HIGHEST)
    grad_premises = dprem - SCALE * (vflt + qval)[:, None] * states_f + dhard
    return (loss, grad_states.astype(jnp.bfloat16), grad_premises.astype(jnp.bfloat16))


def solution(mesh):
    return jax.shard_map(
        body,
        mesh=mesh,
        in_specs=(
            P(("loop", "groups"), None),
            P(("loop", "groups"), None),
            P("loop", "groups"),
            P("loop"),
            P("loop", "groups", None),
            P(("loop", "groups")),
        ),
        out_specs=(P(), P(("loop", "groups"), None), P(("loop", "groups"), None)),
        check_vma=False,
    )
```

profile of v0, /device:TPU:16, one launch (start us, length us, event | category | flops | bytes accessed | tf_op | source)
XLA Modules:
  0.0 425.0 jit_solution(1148805048968045579)
XLA Ops:
  7.9 2.2 gather_fusion.1
  10.2 0.7 all-gather.5.cloned.1.call-update
  12.2 1.3 dynamic-slice
  14.2 12.4 %all-reduce = s32[16]{0:T(128)S(1)} all-reduce(s32[16]{0:T(128)S(1)} %bitcast_dynamic-update-slice_fusion), channel_id=1, replica_groups=mesh['loop'=16,'groups'=32] {'loop'}, use_global_device_ids=true, to_apply=%add | all-reduce | flops 16 | bytes 128
  27.4 71.7 %all-gather.9.cloned.1.call-done = bf16[512,1024]{1,0:T(8,128)(2,1)} async-done(((bf16[16,1024]{1,0:T(8,128)(2,1)}), bf16[512,1024]{1,0:T(8,128)(2,1)}) %all-gather.9.cloned.1.call-update) | async-done | bytes 1048592 | tf_op jit(solution)/shard_map/all_gather | solution.py:40
  99.1 0.8 dynamic-slice_select_fusion
  99.9 0.9 gather_fusion.2
  100.8 1.2 fusion.7
  102.0 38.2 %all-gather.5.cloned.1.call-done = bf16[2048,1024]{1,0:T(8,128)(2,1)} async-done(((bf16[128,1024]{1,0:T(8,128)(2,1)}), bf16[2048,1024]{1,0:T(8,128)(2,1)}) %all-gather.5.cloned.1.call-update) | async-done | bytes 4194320 | tf_op jit(solution)/shard_map/all_gather | solution.py:27
  140.1 3.9 select_reduce_fusion
  144.3 1.2 gather_fusion
  146.3 1.0 convolution_multiply_fusion.1
  147.7 3.7 fusion.5
  151.4 100.6 %psum.7 = f32[]{:T(128)} all-reduce(f32[]{:T(128)} %get-tuple-element.170), channel_id=1, replica_groups=mesh['loop'=16,'groups'=32] {'loop','groups'}, use_global_device_ids=true, to_apply=%region_4.5 | all-reduce | flops 1 | bytes 8 | tf_op jit(solution)/shard_map/psum | solution.py:52
  252.7 162.5 %while.16 = (s32[]{:T(128)}, f32[128,1024]{1,0:T(8,128)S(1)}, s32[]{:T(128)}, bf16[128,2048]{1,0:T(8,128)(2,1)S(1)}, bf16[128,1024]{1,0:T(8,128)(2,1)S(1)}, /*in...) while((s32[]{:T(128)}, f32[128,1024]{1,0:T(8,128)S(1)}, ...), condition=%wide.region_6.7_spmd.clone, body=%wide.region_5.6_spmd.clone.sunk | while | flops 34078736 | bytes 2916682 | solution.py:65
  253.0 1.9 collective-permute-start
  254.9 7.9 %collective-permute-done = bf16[128,1024]{1,0:T(8,128)(2,1)S(1)} collective-permute-done((bf16[128,1024]{1,0:T(8,128)(2,1)S(1)}, bf16[128,1024]{1,0:T(8,128)(2,1)S(1)}, u32[]{:S(2)}, u32[]{:S(2)}) %collective-permute-start) | collective-permute-done | bytes 262176 | tf_op jit(solution)/shard_map/while/body/eval_jaxpr/ppermute | solution.py:12
  263.1 1.9 collective-permute-start
  265.0 7.9 %collective-permute-done = bf16[128,1024]{1,0:T(8,128)(2,1)S(1)} collective-permute-done((bf16[128,1024]{1,0:T(8,128)(2,1)S(1)}, bf16[128,1024]{1,0:T(8,128)(2,1)S(1)}, u32[]{:S(2)}, u32[]{:S(2)}) %collective-permute-start) | collective-permute-done | bytes 262176 | tf_op jit(solution)/shard_map/while/body/eval_jaxpr/ppermute | solution.py:12
  273.3 1.9 collective-permute-start
  275.2 7.9 %collective-permute-done = bf16[128,1024]{1,0:T(8,128)(2,1)S(1)} collective-permute-done((bf16[128,1024]{1,0:T(8,128)(2,1)S(1)}, bf16[128,1024]{1,0:T(8,128)(2,1)S(1)}, u32[]{:S(2)}, u32[]{:S(2)}) %collective-permute-start) | collective-permute-done | bytes 262176 | tf_op jit(solution)/shard_map/while/body/eval_jaxpr/ppermute | solution.py:12
  283.4 1.9 collective-permute-start
  285.3 7.9 %collective-permute-done = bf16[128,1024]{1,0:T(8,128)(2,1)S(1)} collective-permute-done((bf16[128,1024]{1,0:T(8,128)(2,1)S(1)}, bf16[128,1024]{1,0:T(8,128)(2,1)S(1)}, u32[]{:S(2)}, u32[]{:S(2)}) %collective-permute-start) | collective-permute-done | bytes 262176 | tf_op jit(solution)/shard_map/while/body/eval_jaxpr/ppermute | solution.py:12
  293.6 1.9 collective-permute-start
  295.5 7.9 %collective-permute-done = bf16[128,1024]{1,0:T(8,128)(2,1)S(1)} collective-permute-done((bf16[128,1024]{1,0:T(8,128)(2,1)S(1)}, bf16[128,1024]{1,0:T(8,128)(2,1)S(1)}, u32[]{:S(2)}, u32[]{:S(2)}) %collective-permute-start) | collective-permute-done | bytes 262176 | tf_op jit(solution)/shard_map/while/body/eval_jaxpr/ppermute | solution.py:12
  303.7 1.9 collective-permute-start
  305.7 7.9 %collective-permute-done = bf16[128,1024]{1,0:T(8,128)(2,1)S(1)} collective-permute-done((bf16[128,1024]{1,0:T(8,128)(2,1)S(1)}, bf16[128,1024]{1,0:T(8,128)(2,1)S(1)}, u32[]{:S(2)}, u32[]{:S(2)}) %collective-permute-start) | collective-permute-done | bytes 262176 | tf_op jit(solution)/shard_map/while/body/eval_jaxpr/ppermute | solution.py:12
  313.9 1.9 collective-permute-start
  315.8 7.9 %collective-permute-done = bf16[128,1024]{1,0:T(8,128)(2,1)S(1)} collective-permute-done((bf16[128,1024]{1,0:T(8,128)(2,1)S(1)}, bf16[128,1024]{1,0:T(8,128)(2,1)S(1)}, u32[]{:S(2)}, u32[]{:S(2)}) %collective-permute-start) | collective-permute-done | bytes 262176 | tf_op jit(solution)/shard_map/while/body/eval_jaxpr/ppermute | solution.py:12
  324.0 1.9 collective-permute-start
  326.0 7.9 %collective-permute-done = bf16[128,1024]{1,0:T(8,128)(2,1)S(1)} collective-permute-done((bf16[128,1024]{1,0:T(8,128)(2,1)S(1)}, bf16[128,1024]{1,0:T(8,128)(2,1)S(1)}, u32[]{:S(2)}, u32[]{:S(2)}) %collective-permute-start) | collective-permute-done | bytes 262176 | tf_op jit(solution)/shard_map/while/body/eval_jaxpr/ppermute | solution.py:12
  334.2 1.9 collective-permute-start
  336.1 7.9 %collective-permute-done = bf16[128,1024]{1,0:T(8,128)(2,1)S(1)} collective-permute-done((bf16[128,1024]{1,0:T(8,128)(2,1)S(1)}, bf16[128,1024]{1,0:T(8,128)(2,1)S(1)}, u32[]{:S(2)}, u32[]{:S(2)}) %collective-permute-start) | collective-permute-done | bytes 262176 | tf_op jit(solution)/shard_map/while/body/eval_jaxpr/ppermute | solution.py:12
  344.4 1.9 collective-permute-start
  346.3 7.9 %collective-permute-done = bf16[128,1024]{1,0:T(8,128)(2,1)S(1)} collective-permute-done((bf16[128,1024]{1,0:T(8,128)(2,1)S(1)}, bf16[128,1024]{1,0:T(8,128)(2,1)S(1)}, u32[]{:S(2)}, u32[]{:S(2)}) %collective-permute-start) | collective-permute-done | bytes 262176 | tf_op jit(solution)/shard_map/while/body/eval_jaxpr/ppermute | solution.py:12
  354.5 1.9 collective-permute-start
  356.4 7.9 %collective-permute-done = bf16[128,1024]{1,0:T(8,128)(2,1)S(1)} collective-permute-done((bf16[128,1024]{1,0:T(8,128)(2,1)S(1)}, bf16[128,1024]{1,0:T(8,128)(2,1)S(1)}, u32[]{:S(2)}, u32[]{:S(2)}) %collective-permute-start) | collective-permute-done | bytes 262176 | tf_op jit(solution)/shard_map/while/body/eval_jaxpr/ppermute | solution.py:12
  364.7 1.9 collective-permute-start
  366.6 7.9 %collective-permute-done = bf16[128,1024]{1,0:T(8,128)(2,1)S(1)} collective-permute-done((bf16[128,1024]{1,0:T(8,128)(2,1)S(1)}, bf16[128,1024]{1,0:T(8,128)(2,1)S(1)}, u32[]{:S(2)}, u32[]{:S(2)}) %collective-permute-start) | collective-permute-done | bytes 262176 | tf_op jit(solution)/shard_map/while/body/eval_jaxpr/ppermute | solution.py:12
  374.8 1.9 collective-permute-start
  376.7 7.9 %collective-permute-done = bf16[128,1024]{1,0:T(8,128)(2,1)S(1)} collective-permute-done((bf16[128,1024]{1,0:T(8,128)(2,1)S(1)}, bf16[128,1024]{1,0:T(8,128)(2,1)S(1)}, u32[]{:S(2)}, u32[]{:S(2)}) %collective-permute-start) | collective-permute-done | bytes 262176 | tf_op jit(solution)/shard_map/while/body/eval_jaxpr/ppermute | solution.py:12
  385.0 1.9 collective-permute-start
  386.9 7.9 %collective-permute-done = bf16[128,1024]{1,0:T(8,128)(2,1)S(1)} collective-permute-done((bf16[128,1024]{1,0:T(8,128)(2,1)S(1)}, bf16[128,1024]{1,0:T(8,128)(2,1)S(1)}, u32[]{:S(2)}, u32[]{:S(2)}) %collective-permute-start) | collective-permute-done | bytes 262176 | tf_op jit(solution)/shard_map/while/body/eval_jaxpr/ppermute | solution.py:12
  395.1 1.9 collective-permute-start
  397.1 7.9 %collective-permute-done = bf16[128,1024]{1,0:T(8,128)(2,1)S(1)} collective-permute-done((bf16[128,1024]{1,0:T(8,128)(2,1)S(1)}, bf16[128,1024]{1,0:T(8,128)(2,1)S(1)}, u32[]{:S(2)}, u32[]{:S(2)}) %collective-permute-start) | collective-permute-done | bytes 262176 | tf_op jit(solution)/shard_map/while/body/eval_jaxpr/ppermute | solution.py:12
  405.3 1.9 collective-permute-start
  407.2 7.9 %collective-permute-done = bf16[128,1024]{1,0:T(8,128)(2,1)S(1)} collective-permute-done((bf16[128,1024]{1,0:T(8,128)(2,1)S(1)}, bf16[128,1024]{1,0:T(8,128)(2,1)S(1)}, u32[]{:S(2)}, u32[]{:S(2)}) %collective-permute-start) | collective-permute-done | bytes 262176 | tf_op jit(solution)/shard_map/while/body/eval_jaxpr/ppermute | solution.py:12
  415.2 2.1 fusion.6
  (60 shorter events, 8.4 us)
Async XLA Ops:
  7.2 91.9 %all-gather.9.cloned.1.call-start = ((), (), s32[]{:S(2)}) async-start(), calls=%async_computation.2 | async-start | bytes 1081344 | tf_op jit(solution)/shard_map/all_gather | solution.py:40
  10.1 130.0 %all-gather.5.cloned.1.call-start = ((), (), s32[]{:S(2)}) async-start(), calls=%async_computation | async-start | bytes 4456448 | tf_op jit(solution)/shard_map/all_gather | solution.py:27
  10.9 404.3 %all-gather.7.cloned.1.call-start = ((), (), s32[]{:S(2)}) async-start(), calls=%async_computation.1 | async-start | bytes 2162688 | tf_op jit(solution)/shard_map/all_gather | solution.py:68
  100.8 45.5 %copy-start = (bf16[128,1024]{1,0:T(8,128)(2,1)S(1)}, bf16[128,1024]{1,0:T(8,128)(2,1)}, u32[]{:S(2)}) copy-start(bf16[128,1024]{1,0:T(8,128)(2,1)} %param.8) | copy-start | bytes 786436
  100.8 45.5 %copy-start.2 = (s32[128]{0:T(128)S(1)}, s32[128]{0:T(128)}, u32[]{:S(2)}) copy-start(s32[128]{0:T(128)} %param.13) | copy-start | bytes 1540
  102.0 45.7 %copy-start.1 = (bf16[128,1024]{1,0:T(8,128)(2,1)S(1)}, bf16[128,1024]{1,0:T(8,128)(2,1)}, u32[]{:S(2)}) copy-start(bf16[128,1024]{1,0:T(8,128)(2,1)} %param.9) | copy-start | bytes 786436
  252.6 162.5 %copy-start.3 = (s32[1,1,16]{2,1,0:T(1,128)S(1)}, s32[1,1,16]{2,1,0:T(1,128)}, u32[]{:S(2)}) copy-start(s32[1,1,16]{2,1,0:T(1,128)} %param.12) | copy-start | bytes 196
  253.0 9.8 %collective-permute-start = (bf16[128,1024]{1,0:T(8,128)(2,1)S(1)}, bf16[128,1024]{1,0:T(8,128)(2,1)S(1)}, u32[]{:S(2)}, u32[]{:S(2)}) collective-permute-start(bf16[128,1024]{1,0:T(8,128)(2,1)S(1)} %fusion.36), channel_id=1, source_target_pairs={{0,32},{32,64},{64,96},{96,128},{128,160},{160,192},{192,224},{224... | collective-permute-start | bytes 786440 | tf_op jit(solution)/shard_map/while/body/eval_jaxpr/ppermute | solution.py:12
  263.1 9.8 %collective-permute-start = (bf16[128,1024]{1,0:T(8,128)(2,1)S(1)}, bf16[128,1024]{1,0:T(8,128)(2,1)S(1)}, u32[]{:S(2)}, u32[]{:S(2)}) collective-permute-start(bf16[128,1024]{1,0:T(8,128)(2,1)S(1)} %fusion.36), channel_id=1, source_target_pairs={{0,32},{32,64},{64,96},{96,128},{128,160},{160,192},{192,224},{224... | collective-permute-start | bytes 786440 | tf_op jit(solution)/shard_map/while/body/eval_jaxpr/ppermute | solution.py:12
  273.3 9.8 %collective-permute-start = (bf16[128,1024]{1,0:T(8,128)(2,1)S(1)}, bf16[128,1024]{1,0:T(8,128)(2,1)S(1)}, u32[]{:S(2)}, u32[]{:S(2)}) collective-permute-start(bf16[128,1024]{1,0:T(8,128)(2,1)S(1)} %fusion.36), channel_id=1, source_target_pairs={{0,32},{32,64},{64,96},{96,128},{128,160},{160,192},{192,224},{224... | collective-permute-start | bytes 786440 | tf_op jit(solution)/shard_map/while/body/eval_jaxpr/ppermute | solution.py:12
  283.4 9.8 %collective-permute-start = (bf16[128,1024]{1,0:T(8,128)(2,1)S(1)}, bf16[128,1024]{1,0:T(8,128)(2,1)S(1)}, u32[]{:S(2)}, u32[]{:S(2)}) collective-permute-start(bf16[128,1024]{1,0:T(8,128)(2,1)S(1)} %fusion.36), channel_id=1, source_target_pairs={{0,32},{32,64},{64,96},{96,128},{128,160},{160,192},{192,224},{224... | collective-permute-start | bytes 786440 | tf_op jit(solution)/shard_map/while/body/eval_jaxpr/ppermute | solution.py:12
  293.6 9.8 %collective-permute-start = (bf16[128,1024]{1,0:T(8,128)(2,1)S(1)}, bf16[128,1024]{1,0:T(8,128)(2,1)S(1)}, u32[]{:S(2)}, u32[]{:S(2)}) collective-permute-start(bf16[128,1024]{1,0:T(8,128)(2,1)S(1)} %fusion.36), channel_id=1, source_target_pairs={{0,32},{32,64},{64,96},{96,128},{128,160},{160,192},{192,224},{224... | collective-permute-start | bytes 786440 | tf_op jit(solution)/shard_map/while/body/eval_jaxpr/ppermute | solution.py:12
  303.7 9.8 %collective-permute-start = (bf16[128,1024]{1,0:T(8,128)(2,1)S(1)}, bf16[128,1024]{1,0:T(8,128)(2,1)S(1)}, u32[]{:S(2)}, u32[]{:S(2)}) collective-permute-start(bf16[128,1024]{1,0:T(8,128)(2,1)S(1)} %fusion.36), channel_id=1, source_target_pairs={{0,32},{32,64},{64,96},{96,128},{128,160},{160,192},{192,224},{224... | collective-permute-start | bytes 786440 | tf_op jit(solution)/shard_map/while/body/eval_jaxpr/ppermute | solution.py:12
  313.9 9.8 %collective-permute-start = (bf16[128,1024]{1,0:T(8,128)(2,1)S(1)}, bf16[128,1024]{1,0:T(8,128)(2,1)S(1)}, u32[]{:S(2)}, u32[]{:S(2)}) collective-permute-start(bf16[128,1024]{1,0:T(8,128)(2,1)S(1)} %fusion.36), channel_id=1, source_target_pairs={{0,32},{32,64},{64,96},{96,128},{128,160},{160,192},{192,224},{224... | collective-permute-start | bytes 786440 | tf_op jit(solution)/shard_map/while/body/eval_jaxpr/ppermute | solution.py:12
  324.0 9.8 %collective-permute-start = (bf16[128,1024]{1,0:T(8,128)(2,1)S(1)}, bf16[128,1024]{1,0:T(8,128)(2,1)S(1)}, u32[]{:S(2)}, u32[]{:S(2)}) collective-permute-start(bf16[128,1024]{1,0:T(8,128)(2,1)S(1)} %fusion.36), channel_id=1, source_target_pairs={{0,32},{32,64},{64,96},{96,128},{128,160},{160,192},{192,224},{224... | collective-permute-start | bytes 786440 | tf_op jit(solution)/shard_map/while/body/eval_jaxpr/ppermute | solution.py:12
  334.2 9.8 %collective-permute-start = (bf16[128,1024]{1,0:T(8,128)(2,1)S(1)}, bf16[128,1024]{1,0:T(8,128)(2,1)S(1)}, u32[]{:S(2)}, u32[]{:S(2)}) collective-permute-start(bf16[128,1024]{1,0:T(8,128)(2,1)S(1)} %fusion.36), channel_id=1, source_target_pairs={{0,32},{32,64},{64,96},{96,128},{128,160},{160,192},{192,224},{224... | collective-permute-start | bytes 786440 | tf_op jit(solution)/shard_map/while/body/eval_jaxpr/ppermute | solution.py:12
  344.4 9.8 %collective-permute-start = (bf16[128,1024]{1,0:T(8,128)(2,1)S(1)}, bf16[128,1024]{1,0:T(8,128)(2,1)S(1)}, u32[]{:S(2)}, u32[]{:S(2)}) collective-permute-start(bf16[128,1024]{1,0:T(8,128)(2,1)S(1)} %fusion.36), channel_id=1, source_target_pairs={{0,32},{32,64},{64,96},{96,128},{128,160},{160,192},{192,224},{224... | collective-permute-start | bytes 786440 | tf_op jit(solution)/shard_map/while/body/eval_jaxpr/ppermute | solution.py:12
  354.5 9.8 %collective-permute-start = (bf16[128,1024]{1,0:T(8,128)(2,1)S(1)}, bf16[128,1024]{1,0:T(8,128)(2,1)S(1)}, u32[]{:S(2)}, u32[]{:S(2)}) collective-permute-start(bf16[128,1024]{1,0:T(8,128)(2,1)S(1)} %fusion.36), channel_id=1, source_target_pairs={{0,32},{32,64},{64,96},{96,128},{128,160},{160,192},{192,224},{224... | collective-permute-start | bytes 786440 | tf_op jit(solution)/shard_map/while/body/eval_jaxpr/ppermute | solution.py:12
  364.7 9.8 %collective-permute-start = (bf16[128,1024]{1,0:T(8,128)(2,1)S(1)}, bf16[128,1024]{1,0:T(8,128)(2,1)S(1)}, u32[]{:S(2)}, u32[]{:S(2)}) collective-permute-start(bf16[128,1024]{1,0:T(8,128)(2,1)S(1)} %fusion.36), channel_id=1, source_target_pairs={{0,32},{32,64},{64,96},{96,128},{128,160},{160,192},{192,224},{224... | collective-permute-start | bytes 786440 | tf_op jit(solution)/shard_map/while/body/eval_jaxpr/ppermute | solution.py:12
  374.8 9.8 %collective-permute-start = (bf16[128,1024]{1,0:T(8,128)(2,1)S(1)}, bf16[128,1024]{1,0:T(8,128)(2,1)S(1)}, u32[]{:S(2)}, u32[]{:S(2)}) collective-permute-start(bf16[128,1024]{1,0:T(8,128)(2,1)S(1)} %fusion.36), channel_id=1, source_target_pairs={{0,32},{32,64},{64,96},{96,128},{128,160},{160,192},{192,224},{224... | collective-permute-start | bytes 786440 | tf_op jit(solution)/shard_map/while/body/eval_jaxpr/ppermute | solution.py:12
  385.0 9.8 %collective-permute-start = (bf16[128,1024]{1,0:T(8,128)(2,1)S(1)}, bf16[128,1024]{1,0:T(8,128)(2,1)S(1)}, u32[]{:S(2)}, u32[]{:S(2)}) collective-permute-start(bf16[128,1024]{1,0:T(8,128)(2,1)S(1)} %fusion.36), channel_id=1, source_target_pairs={{0,32},{32,64},{64,96},{96,128},{128,160},{160,192},{192,224},{224... | collective-permute-start | bytes 786440 | tf_op jit(solution)/shard_map/while/body/eval_jaxpr/ppermute | solution.py:12
  395.1 9.8 %collective-permute-start = (bf16[128,1024]{1,0:T(8,128)(2,1)S(1)}, bf16[128,1024]{1,0:T(8,128)(2,1)S(1)}, u32[]{:S(2)}, u32[]{:S(2)}) collective-permute-start(bf16[128,1024]{1,0:T(8,128)(2,1)S(1)} %fusion.36), channel_id=1, source_target_pairs={{0,32},{32,64},{64,96},{96,128},{128,160},{160,192},{192,224},{224... | collective-permute-start | bytes 786440 | tf_op jit(solution)/shard_map/while/body/eval_jaxpr/ppermute | solution.py:12
  405.3 9.8 %collective-permute-start = (bf16[128,1024]{1,0:T(8,128)(2,1)S(1)}, bf16[128,1024]{1,0:T(8,128)(2,1)S(1)}, u32[]{:S(2)}, u32[]{:S(2)}) collective-permute-start(bf16[128,1024]{1,0:T(8,128)(2,1)S(1)} %fusion.36), channel_id=1, source_target_pairs={{0,32},{32,64},{64,96},{96,128},{128,160},{160,192},{192,224},{224... | collective-permute-start | bytes 786440 | tf_op jit(solution)/shard_map/while/body/eval_jaxpr/ppermute | solution.py:12
Sparse Core Ops, SparseCore 0:
  11.7 87.3 all-gather.8
  101.2 38.8 all-gather.4
  147.5 86.5 all-gather.6
where the time goes:
time: 426 us; the launch traced here: 425 us
  waiting for transfers between devices  237 us (56%)
  blocking collectives  113 us (27%)
  starting transfers between devices  30.8 us (7%)
  between operations  17 us (4%)
  matrix products  14.9 us (3%)
  local copies, waits for them, and re-layouts  6.3 us (1%)
  other arithmetic  5.34 us (1%)
    ppermute x16, waiting for transfers between devices, from_behind(): return lax.ppermute(value, axis, pairs)  126 us
    psum x1, blocking collectives, body(): lax.psum(jnp.sum(terms), ('loop', 'groups'))  101 us
    all_gather x1, waiting for transfers between devices, body(): piece = lax.all_gather(offered, 'groups', axis=0, tiled=True)  71.7 us
    all_gather x1, waiting for transfers between devices, body(): lax.all_gather(premises, 'loop', axis=0, tiled=True)  38.2 us
    ppermute x16, starting transfers between devices, from_behind(): return lax.ppermute(value, axis, pairs)  30.7 us
    unnamed x1, blocking collectives  12.4 us
  transfers between devices with their start and end apart: 19, of which 18 were waited for; matrix products, arithmetic and copies ran while one was open for 3% of the time, Pallas kernels for 0%

commit v1 on v0

--- a/solution.py
+++ b/solution.py
@@ -24,7 +24,9 @@
     vflt = valid.astype(jnp.float32)
     partner = jnp.bitwise_xor(group, partner_mask[0])
     keys, counts_all = (
-        lax.all_gather(premises, "loop", axis=0, tiled=True),
+        jnp.concatenate(
+            lax.all_to_all(jnp.stack([premises] * lax.axis_size("loop")), "loop", 0, 0), axis=0
+        ),
         lax.all_gather(counts, "loop", axis=0, tiled=True),
     )
     column = jnp.arange(loop_size * rows, dtype=jnp.int32)

time: 426 us -> 392 us (0.920)
  waiting for transfers between devices: 237 us -> 161 us
  blocking collectives: 113 us -> 149 us
  starting transfers between devices: 30.8 us -> 36.4 us
    unnamed x1, blocking collectives: 12.4 us -> 51.9 us
    all_gather x1 -> x0, waiting for transfers between devices: 38.2 us -> none  [body(): lax.all_gather(premises, 'loop', axis=0, tiled=True)]
    all_gather x1, waiting for transfers between devices: 71.7 us -> 34.7 us  [body(): piece = lax.all_gather(offered, 'groups', axis=0, tiled=True)]
    all_to_all x0 -> x1, starting transfers between devices: none -> 5.61 us  [body(): lax.all_to_all(jnp.stack([premises] * lax.axis_size('loop')), 'loop', 0, 0)]
  transfers between devices with their start and end apart: 19 -> 19, of which waited for: 18 -> 17; matrix products, arithmetic and copies ran while one was open for 3% -> 4% of each run, Pallas kernels for 0% -> 0%
where the time goes in v1:
time: 392 us; the launch traced here: 391 us
  waiting for transfers between devices  161 us (41%)
  blocking collectives  149 us (38%)
  starting transfers between devices  36.4 us (9%)
  between operations  17.3 us (4%)
  matrix products  14.9 us (4%)
  local copies, waits for them, and re-layouts  8.74 us (2%)
    ppermute x16, waiting for transfers between devices, from_behind(): return lax.ppermute(value, axis, pairs)  126 us
    psum x1, blocking collectives, body(): lax.psum(jnp.sum(terms), ('loop', 'groups'))  96.9 us
    unnamed x1, blocking collectives  51.9 us
    all_gather x1, waiting for transfers between devices, body(): piece = lax.all_gather(offered, 'groups', axis=0, tiled=True)  34.7 us
    ppermute x16, starting transfers between devices, from_behind(): return lax.ppermute(value, axis, pairs)  30.7 us
  transfers between devices with their start and end apart: 19, of which 17 were waited for; matrix products, arithmetic and copies ran while one was open for 4% of the time, Pallas kernels for 0%

profile of v1, /device:TPU:16, one launch (start us, length us, event | category | flops | bytes accessed | tf_op | source)
XLA Modules:
  0.0 390.8 jit_solution(3097697219827720423)
XLA Ops:
  7.2 3.5 stack.2
  10.6 5.6 %all-to-all-start = ((bf16[16,128,1024]{2,1,0:T(8,128)(2,1)}), bf16[16,128,1024]{2,1,0:T(8,128)(2,1)}, u32[]{:S(2)}, u32[]{:S(2)}) async-start(bf16[16,128,1024]{2,1,0:T(8,128)(2,1)} %stack.2), calls=%async_computation | async-start | bytes 8388608 | tf_op jit(solution)/shard_map/all_to_all | solution.py:28
  16.3 1.2 gather_fusion.1
  19.0 1.3 dynamic-slice
  20.2 0.7 bitcast_dynamic-update-slice_fusion
  20.9 51.9 %all-reduce = s32[16]{0:T(128)S(1)} all-reduce(s32[16]{0:T(128)S(1)} %bitcast_dynamic-update-slice_fusion), channel_id=1, replica_groups=mesh['loop'=16,'groups'=32] {'loop'}, use_global_device_ids=true, to_apply=%add | all-reduce | flops 16 | bytes 128
  72.9 34.7 %all-gather.6.cloned.1.call-done = bf16[512,1024]{1,0:T(8,128)(2,1)} async-done(((bf16[16,1024]{1,0:T(8,128)(2,1)}), bf16[512,1024]{1,0:T(8,128)(2,1)}) %all-gather.6.cloned.1.call-update) | async-done | bytes 1048592 | tf_op jit(solution)/shard_map/all_gather | solution.py:42
  107.6 0.8 dynamic-slice_select_fusion
  108.5 0.9 gather_fusion.2
  109.5 3.8 select_reduce_fusion
  113.6 1.2 gather_fusion
  115.5 1.0 convolution_multiply_fusion.1
  116.9 3.7 fusion.5
  120.6 96.9 %psum.7 = f32[]{:T(128)} all-reduce(f32[]{:T(128)} %get-tuple-element.170), channel_id=1, replica_groups=mesh['loop'=16,'groups'=32] {'loop','groups'}, use_global_device_ids=true, to_apply=%region_4.5 | all-reduce | flops 1 | bytes 8 | tf_op jit(solution)/shard_map/psum | solution.py:54
  218.1 162.5 %while.16 = (s32[]{:T(128)}, f32[128,1024]{1,0:T(8,128)S(1)}, s32[]{:T(128)}, bf16[128,2048]{1,0:T(8,128)(2,1)S(1)}, bf16[128,1024]{1,0:T(8,128)(2,1)S(1)}, /*in...) while((s32[]{:T(128)}, f32[128,1024]{1,0:T(8,128)S(1)}, ...), condition=%wide.region_6.7_spmd.clone, body=%wide.region_5.6_spmd.clone.sunk | while | flops 34078736 | bytes 2916682 | solution.py:67
  218.5 1.9 collective-permute-start
  220.4 7.9 %collective-permute-done = bf16[128,1024]{1,0:T(8,128)(2,1)S(1)} collective-permute-done((bf16[128,1024]{1,0:T(8,128)(2,1)S(1)}, bf16[128,1024]{1,0:T(8,128)(2,1)S(1)}, u32[]{:S(2)}, u32[]{:S(2)}) %collective-permute-start) | collective-permute-done | bytes 262176 | tf_op jit(solution)/shard_map/while/body/eval_jaxpr/ppermute | solution.py:12
  228.6 1.9 collective-permute-start
  230.5 7.9 %collective-permute-done = bf16[128,1024]{1,0:T(8,128)(2,1)S(1)} collective-permute-done((bf16[128,1024]{1,0:T(8,128)(2,1)S(1)}, bf16[128,1024]{1,0:T(8,128)(2,1)S(1)}, u32[]{:S(2)}, u32[]{:S(2)}) %collective-permute-start) | collective-permute-done | bytes 262176 | tf_op jit(solution)/shard_map/while/body/eval_jaxpr/ppermute | solution.py:12
  238.8 1.9 collective-permute-start
  240.7 7.9 %collective-permute-done = bf16[128,1024]{1,0:T(8,128)(2,1)S(1)} collective-permute-done((bf16[128,1024]{1,0:T(8,128)(2,1)S(1)}, bf16[128,1024]{1,0:T(8,128)(2,1)S(1)}, u32[]{:S(2)}, u32[]{:S(2)}) %collective-permute-start) | collective-permute-done | bytes 262176 | tf_op jit(solution)/shard_map/while/body/eval_jaxpr/ppermute | solution.py:12
  248.9 1.9 collective-permute-start
  250.8 7.9 %collective-permute-done = bf16[128,1024]{1,0:T(8,128)(2,1)S(1)} collective-permute-done((bf16[128,1024]{1,0:T(8,128)(2,1)S(1)}, bf16[128,1024]{1,0:T(8,128)(2,1)S(1)}, u32[]{:S(2)}, u32[]{:S(2)}) %collective-permute-start) | collective-permute-done | bytes 262176 | tf_op jit(solution)/shard_map/while/body/eval_jaxpr/ppermute | solution.py:12
  259.1 1.9 collective-permute-start
  261.0 7.9 %collective-permute-done = bf16[128,1024]{1,0:T(8,128)(2,1)S(1)} collective-permute-done((bf16[128,1024]{1,0:T(8,128)(2,1)S(1)}, bf16[128,1024]{1,0:T(8,128)(2,1)S(1)}, u32[]{:S(2)}, u32[]{:S(2)}) %collective-permute-start) | collective-permute-done | bytes 262176 | tf_op jit(solution)/shard_map/while/body/eval_jaxpr/ppermute | solution.py:12
  269.2 1.9 collective-permute-start
  271.1 7.9 %collective-permute-done = bf16[128,1024]{1,0:T(8,128)(2,1)S(1)} collective-permute-done((bf16[128,1024]{1,0:T(8,128)(2,1)S(1)}, bf16[128,1024]{1,0:T(8,128)(2,1)S(1)}, u32[]{:S(2)}, u32[]{:S(2)}) %collective-permute-start) | collective-permute-done | bytes 262176 | tf_op jit(solution)/shard_map/while/body/eval_jaxpr/ppermute | solution.py:12
  279.4 1.9 collective-permute-start
  281.3 7.9 %collective-permute-done = bf16[128,1024]{1,0:T(8,128)(2,1)S(1)} collective-permute-done((bf16[128,1024]{1,0:T(8,128)(2,1)S(1)}, bf16[128,1024]{1,0:T(8,128)(2,1)S(1)}, u32[]{:S(2)}, u32[]{:S(2)}) %collective-permute-start) | collective-permute-done | bytes 262176 | tf_op jit(solution)/shard_map/while/body/eval_jaxpr/ppermute | solution.py:12
  289.5 1.9 collective-permute-start
  291.5 7.9 %collective-permute-done = bf16[128,1024]{1,0:T(8,128)(2,1)S(1)} collective-permute-done((bf16[128,1024]{1,0:T(8,128)(2,1)S(1)}, bf16[128,1024]{1,0:T(8,128)(2,1)S(1)}, u32[]{:S(2)}, u32[]{:S(2)}) %collective-permute-start) | collective-permute-done | bytes 262176 | tf_op jit(solution)/shard_map/while/body/eval_jaxpr/ppermute | solution.py:12
  299.7 1.9 collective-permute-start
  301.6 7.9 %collective-permute-done = bf16[128,1024]{1,0:T(8,128)(2,1)S(1)} collective-permute-done((bf16[128,1024]{1,0:T(8,128)(2,1)S(1)}, bf16[128,1024]{1,0:T(8,128)(2,1)S(1)}, u32[]{:S(2)}, u32[]{:S(2)}) %collective-permute-start) | collective-permute-done | bytes 262176 | tf_op jit(solution)/shard_map/while/body/eval_jaxpr/ppermute | solution.py:12
  309.8 1.9 collective-permute-start
  311.8 7.9 %collective-permute-done = bf16[128,1024]{1,0:T(8,128)(2,1)S(1)} collective-permute-done((bf16[128,1024]{1,0:T(8,128)(2,1)S(1)}, bf16[128,1024]{1,0:T(8,128)(2,1)S(1)}, u32[]{:S(2)}, u32[]{:S(2)}) %collective-permute-start) | collective-permute-done | bytes 262176 | tf_op jit(solution)/shard_map/while/body/eval_jaxpr/ppermute | solution.py:12
  320.0 1.9 collective-permute-start
  321.9 7.9 %collective-permute-done = bf16[128,1024]{1,0:T(8,128)(2,1)S(1)} collective-permute-done((bf16[128,1024]{1,0:T(8,128)(2,1)S(1)}, bf16[128,1024]{1,0:T(8,128)(2,1)S(1)}, u32[]{:S(2)}, u32[]{:S(2)}) %collective-permute-start) | collective-permute-done | bytes 262176 | tf_op jit(solution)/shard_map/while/body/eval_jaxpr/ppermute | solution.py:12
  330.2 1.9 collective-permute-start
  332.1 7.9 %collective-permute-done = bf16[128,1024]{1,0:T(8,128)(2,1)S(1)} collective-permute-done((bf16[128,1024]{1,0:T(8,128)(2,1)S(1)}, bf16[128,1024]{1,0:T(8,128)(2,1)S(1)}, u32[]{:S(2)}, u32[]{:S(2)}) %collective-permute-start) | collective-permute-done | bytes 262176 | tf_op jit(solution)/shard_map/while/body/eval_jaxpr/ppermute | solution.py:12
  340.3 1.9 collective-permute-start
  342.2 7.9 %collective-permute-done = bf16[128,1024]{1,0:T(8,128)(2,1)S(1)} collective-permute-done((bf16[128,1024]{1,0:T(8,128)(2,1)S(1)}, bf16[128,1024]{1,0:T(8,128)(2,1)S(1)}, u32[]{:S(2)}, u32[]{:S(2)}) %collective-permute-start) | collective-permute-done | bytes 262176 | tf_op jit(solution)/shard_map/while/body/eval_jaxpr/ppermute | solution.py:12
  350.5 1.9 collective-permute-start
  352.4 7.9 %collective-permute-done = bf16[128,1024]{1,0:T(8,128)(2,1)S(1)} collective-permute-done((bf16[128,1024]{1,0:T(8,128)(2,1)S(1)}, bf16[128,1024]{1,0:T(8,128)(2,1)S(1)}, u32[]{:S(2)}, u32[]{:S(2)}) %collective-permute-start) | collective-permute-done | bytes 262176 | tf_op jit(solution)/shard_map/while/body/eval_jaxpr/ppermute | solution.py:12
  360.6 1.9 collective-permute-start
  362.6 7.9 %collective-permute-done = bf16[128,1024]{1,0:T(8,128)(2,1)S(1)} collective-permute-done((bf16[128,1024]{1,0:T(8,128)(2,1)S(1)}, bf16[128,1024]{1,0:T(8,128)(2,1)S(1)}, u32[]{:S(2)}, u32[]{:S(2)}) %collective-permute-start) | collective-permute-done | bytes 262176 | tf_op jit(solution)/shard_map/while/body/eval_jaxpr/ppermute | solution.py:12
  370.8 1.9 collective-permute-start
  372.7 7.9 %collective-permute-done = bf16[128,1024]{1,0:T(8,128)(2,1)S(1)} collective-permute-done((bf16[128,1024]{1,0:T(8,128)(2,1)S(1)}, bf16[128,1024]{1,0:T(8,128)(2,1)S(1)}, u32[]{:S(2)}, u32[]{:S(2)}) %collective-permute-start) | collective-permute-done | bytes 262176 | tf_op jit(solution)/shard_map/while/body/eval_jaxpr/ppermute | solution.py:12
  380.7 2.1 fusion.6
  (60 shorter events, 6.5 us)
Async XLA Ops:
  10.6 5.7 %copy-start.3 = (s32[1,1,16]{2,1,0:T(1,128)S(1)}, s32[1,1,16]{2,1,0:T(1,128)}, u32[]{:S(2)}) copy-start(s32[1,1,16]{2,1,0:T(1,128)} %param.12) | copy-start | bytes 196
  10.6 5.7 %copy-start.1 = (bf16[128,1024]{1,0:T(8,128)(2,1)S(1)}, bf16[128,1024]{1,0:T(8,128)(2,1)}, u32[]{:S(2)}) copy-start(bf16[128,1024]{1,0:T(8,128)(2,1)} %param.9) | copy-start | bytes 786436
  10.6 62.2 %copy-start.2 = (s32[128]{0:T(128)S(1)}, s32[128]{0:T(128)}, u32[]{:S(2)}) copy-start(s32[128]{0:T(128)} %param.13) | copy-start | bytes 1540
  10.6 98.7 %copy-start = (bf16[128,1024]{1,0:T(8,128)(2,1)S(1)}, bf16[128,1024]{1,0:T(8,128)(2,1)}, u32[]{:S(2)}) copy-start(bf16[128,1024]{1,0:T(8,128)(2,1)} %param.8) | copy-start | bytes 786436
  10.6 98.9 %all-to-all-start = ((bf16[16,128,1024]{2,1,0:T(8,128)(2,1)}), bf16[16,128,1024]{2,1,0:T(8,128)(2,1)}, u32[]{:S(2)}, u32[]{:S(2)}) async-start(bf16[16,128,1024]{2,1,0:T(8,128)(2,1)} %stack.2), calls=%async_computation | async-start | bytes 8388608 | tf_op jit(solution)/shard_map/all_to_all | solution.py:28
  16.2 91.4 %all-gather.6.cloned.1.call-start = ((), (), s32[]{:S(2)}) async-start(), calls=%async_computation.2 | async-start | bytes 1081344 | tf_op jit(solution)/shard_map/all_gather | solution.py:42
  17.6 363.1 %all-gather.4.cloned.1.call-start = ((), (), s32[]{:S(2)}) async-start(), calls=%async_computation.1 | async-start | bytes 2162688 | tf_op jit(solution)/shard_map/all_gather | solution.py:70
  218.5 9.8 %collective-permute-start = (bf16[128,1024]{1,0:T(8,128)(2,1)S(1)}, bf16[128,1024]{1,0:T(8,128)(2,1)S(1)}, u32[]{:S(2)}, u32[]{:S(2)}) collective-permute-start(bf16[128,1024]{1,0:T(8,128)(2,1)S(1)} %fusion.36), channel_id=1, source_target_pairs={{0,32},{32,64},{64,96},{96,128},{128,160},{160,192},{192,224},{224... | collective-permute-start | bytes 786440 | tf_op jit(solution)/shard_map/while/body/eval_jaxpr/ppermute | solution.py:12
  228.6 9.8 %collective-permute-start = (bf16[128,1024]{1,0:T(8,128)(2,1)S(1)}, bf16[128,1024]{1,0:T(8,128)(2,1)S(1)}, u32[]{:S(2)}, u32[]{:S(2)}) collective-permute-start(bf16[128,1024]{1,0:T(8,128)(2,1)S(1)} %fusion.36), channel_id=1, source_target_pairs={{0,32},{32,64},{64,96},{96,128},{128,160},{160,192},{192,224},{224... | collective-permute-start | bytes 786440 | tf_op jit(solution)/shard_map/while/body/eval_jaxpr/ppermute | solution.py:12
  238.8 9.8 %collective-permute-start = (bf16[128,1024]{1,0:T(8,128)(2,1)S(1)}, bf16[128,1024]{1,0:T(8,128)(2,1)S(1)}, u32[]{:S(2)}, u32[]{:S(2)}) collective-permute-start(bf16[128,1024]{1,0:T(8,128)(2,1)S(1)} %fusion.36), channel_id=1, source_target_pairs={{0,32},{32,64},{64,96},{96,128},{128,160},{160,192},{192,224},{224... | collective-permute-start | bytes 786440 | tf_op jit(solution)/shard_map/while/body/eval_jaxpr/ppermute | solution.py:12
  248.9 9.8 %collective-permute-start = (bf16[128,1024]{1,0:T(8,128)(2,1)S(1)}, bf16[128,1024]{1,0:T(8,128)(2,1)S(1)}, u32[]{:S(2)}, u32[]{:S(2)}) collective-permute-start(bf16[128,1024]{1,0:T(8,128)(2,1)S(1)} %fusion.36), channel_id=1, source_target_pairs={{0,32},{32,64},{64,96},{96,128},{128,160},{160,192},{192,224},{224... | collective-permute-start | bytes 786440 | tf_op jit(solution)/shard_map/while/body/eval_jaxpr/ppermute | solution.py:12
  259.1 9.8 %collective-permute-start = (bf16[128,1024]{1,0:T(8,128)(2,1)S(1)}, bf16[128,1024]{1,0:T(8,128)(2,1)S(1)}, u32[]{:S(2)}, u32[]{:S(2)}) collective-permute-start(bf16[128,1024]{1,0:T(8,128)(2,1)S(1)} %fusion.36), channel_id=1, source_target_pairs={{0,32},{32,64},{64,96},{96,128},{128,160},{160,192},{192,224},{224... | collective-permute-start | bytes 786440 | tf_op jit(solution)/shard_map/while/body/eval_jaxpr/ppermute | solution.py:12
  269.2 9.8 %collective-permute-start = (bf16[128,1024]{1,0:T(8,128)(2,1)S(1)}, bf16[128,1024]{1,0:T(8,128)(2,1)S(1)}, u32[]{:S(2)}, u32[]{:S(2)}) collective-permute-start(bf16[128,1024]{1,0:T(8,128)(2,1)S(1)} %fusion.36), channel_id=1, source_target_pairs={{0,32},{32,64},{64,96},{96,128},{128,160},{160,192},{192,224},{224... | collective-permute-start | bytes 786440 | tf_op jit(solution)/shard_map/while/body/eval_jaxpr/ppermute | solution.py:12
  279.4 9.8 %collective-permute-start = (bf16[128,1024]{1,0:T(8,128)(2,1)S(1)}, bf16[128,1024]{1,0:T(8,128)(2,1)S(1)}, u32[]{:S(2)}, u32[]{:S(2)}) collective-permute-start(bf16[128,1024]{1,0:T(8,128)(2,1)S(1)} %fusion.36), channel_id=1, source_target_pairs={{0,32},{32,64},{64,96},{96,128},{128,160},{160,192},{192,224},{224... | collective-permute-start | bytes 786440 | tf_op jit(solution)/shard_map/while/body/eval_jaxpr/ppermute | solution.py:12
  289.5 9.8 %collective-permute-start = (bf16[128,1024]{1,0:T(8,128)(2,1)S(1)}, bf16[128,1024]{1,0:T(8,128)(2,1)S(1)}, u32[]{:S(2)}, u32[]{:S(2)}) collective-permute-start(bf16[128,1024]{1,0:T(8,128)(2,1)S(1)} %fusion.36), channel_id=1, source_target_pairs={{0,32},{32,64},{64,96},{96,128},{128,160},{160,192},{192,224},{224... | collective-permute-start | bytes 786440 | tf_op jit(solution)/shard_map/while/body/eval_jaxpr/ppermute | solution.py:12
  299.7 9.8 %collective-permute-start = (bf16[128,1024]{1,0:T(8,128)(2,1)S(1)}, bf16[128,1024]{1,0:T(8,128)(2,1)S(1)}, u32[]{:S(2)}, u32[]{:S(2)}) collective-permute-start(bf16[128,1024]{1,0:T(8,128)(2,1)S(1)} %fusion.36), channel_id=1, source_target_pairs={{0,32},{32,64},{64,96},{96,128},{128,160},{160,192},{192,224},{224... | collective-permute-start | bytes 786440 | tf_op jit(solution)/shard_map/while/body/eval_jaxpr/ppermute | solution.py:12
  309.8 9.8 %collective-permute-start = (bf16[128,1024]{1,0:T(8,128)(2,1)S(1)}, bf16[128,1024]{1,0:T(8,128)(2,1)S(1)}, u32[]{:S(2)}, u32[]{:S(2)}) collective-permute-start(bf16[128,1024]{1,0:T(8,128)(2,1)S(1)} %fusion.36), channel_id=1, source_target_pairs={{0,32},{32,64},{64,96},{96,128},{128,160},{160,192},{192,224},{224... | collective-permute-start | bytes 786440 | tf_op jit(solution)/shard_map/while/body/eval_jaxpr/ppermute | solution.py:12
  320.0 9.8 %collective-permute-start = (bf16[128,1024]{1,0:T(8,128)(2,1)S(1)}, bf16[128,1024]{1,0:T(8,128)(2,1)S(1)}, u32[]{:S(2)}, u32[]{:S(2)}) collective-permute-start(bf16[128,1024]{1,0:T(8,128)(2,1)S(1)} %fusion.36), channel_id=1, source_target_pairs={{0,32},{32,64},{64,96},{96,128},{128,160},{160,192},{192,224},{224... | collective-permute-start | bytes 786440 | tf_op jit(solution)/shard_map/while/body/eval_jaxpr/ppermute | solution.py:12
  330.2 9.8 %collective-permute-start = (bf16[128,1024]{1,0:T(8,128)(2,1)S(1)}, bf16[128,1024]{1,0:T(8,128)(2,1)S(1)}, u32[]{:S(2)}, u32[]{:S(2)}) collective-permute-start(bf16[128,1024]{1,0:T(8,128)(2,1)S(1)} %fusion.36), channel_id=1, source_target_pairs={{0,32},{32,64},{64,96},{96,128},{128,160},{160,192},{192,224},{224... | collective-permute-start | bytes 786440 | tf_op jit(solution)/shard_map/while/body/eval_jaxpr/ppermute | solution.py:12
  340.3 9.8 %collective-permute-start = (bf16[128,1024]{1,0:T(8,128)(2,1)S(1)}, bf16[128,1024]{1,0:T(8,128)(2,1)S(1)}, u32[]{:S(2)}, u32[]{:S(2)}) collective-permute-start(bf16[128,1024]{1,0:T(8,128)(2,1)S(1)} %fusion.36), channel_id=1, source_target_pairs={{0,32},{32,64},{64,96},{96,128},{128,160},{160,192},{192,224},{224... | collective-permute-start | bytes 786440 | tf_op jit(solution)/shard_map/while/body/eval_jaxpr/ppermute | solution.py:12
  350.5 9.8 %collective-permute-start = (bf16[128,1024]{1,0:T(8,128)(2,1)S(1)}, bf16[128,1024]{1,0:T(8,128)(2,1)S(1)}, u32[]{:S(2)}, u32[]{:S(2)}) collective-permute-start(bf16[128,1024]{1,0:T(8,128)(2,1)S(1)} %fusion.36), channel_id=1, source_target_pairs={{0,32},{32,64},{64,96},{96,128},{128,160},{160,192},{192,224},{224... | collective-permute-start | bytes 786440 | tf_op jit(solution)/shard_map/while/body/eval_jaxpr/ppermute | solution.py:12
  360.6 9.8 %collective-permute-start = (bf16[128,1024]{1,0:T(8,128)(2,1)S(1)}, bf16[128,1024]{1,0:T(8,128)(2,1)S(1)}, u32[]{:S(2)}, u32[]{:S(2)}) collective-permute-start(bf16[128,1024]{1,0:T(8,128)(2,1)S(1)} %fusion.36), channel_id=1, source_target_pairs={{0,32},{32,64},{64,96},{96,128},{128,160},{160,192},{192,224},{224... | collective-permute-start | bytes 786440 | tf_op jit(solution)/shard_map/while/body/eval_jaxpr/ppermute | solution.py:12
  370.8 9.8 %collective-permute-start = (bf16[128,1024]{1,0:T(8,128)(2,1)S(1)}, bf16[128,1024]{1,0:T(8,128)(2,1)S(1)}, u32[]{:S(2)}, u32[]{:S(2)}) collective-permute-start(bf16[128,1024]{1,0:T(8,128)(2,1)S(1)} %fusion.36), channel_id=1, source_target_pairs={{0,32},{32,64},{64,96},{96,128},{128,160},{160,192},{192,224},{224... | collective-permute-start | bytes 786440 | tf_op jit(solution)/shard_map/while/body/eval_jaxpr/ppermute | solution.py:12
Sparse Core Ops, SparseCore 0:
  20.8 86.7 all-gather.5
  116.7 82.5 all-gather.3
